TPU v7x, 32 devices: a whole 2x2x4 slice. The times are simulated.
32 devices in a mesh: dp: 8 (over z, x), row: 2 (over core), col: 2 (over y).
Axes of the slice: x: 2, y: 2, z: 4, core: 2. Of those that a mesh axis runs over, the one named last changes fastest.
Arguments:
- tokens: bfloat16 [2, 8, 256, 2048], P(None, None, 'dp', ('row', 'col')), may hold values from -57 to 57
- lengths: int32 [2, 8], replicated, may hold values from 64 to 256, as said below
- deal_order: int32 [2, 8], replicated, may hold values from 0 to 7, each once within a row
- attention_gain: float32 [2048], P(('row', 'col')), may hold values from 0.25 to 1.75
- query_weight: bfloat16 [2048, 2048], P('row', 'col'), may hold values from -0.1875 to 0.1875
- key_weight: bfloat16 [2048, 2048], P('row', 'col'), may hold values from -0.1875 to 0.1875
- value_weight: bfloat16 [2048, 2048], P('row', 'col'), may hold values from -0.125 to 0.125
- output_weight: bfloat16 [2048, 2048], P('col', 'row'), may hold values from -0.25 to 0.25
- feed_gain: float32 [2048], P(('row', 'col')), may hold values from 0.25 to 1.75
- gate_weight: bfloat16 [2048, 8192], P('row', 'col'), may hold values from -0.125 to 0.125
- up_weight: bfloat16 [2048, 8192], P('row', 'col'), may hold values from -0.125 to 0.125
- down_weight: bfloat16 [8192, 2048], P('col', 'row'), may hold values from -0.09375 to 0.09375
- cotangent: bfloat16 [2, 8, 256, 2048], P(None, 'dp', None, ('row', 'col')), may hold values from -6 to 6
Outputs:
- layer_output: bfloat16 [2, 8, 256, 2048], P(None, None, 'dp', ('row', 'col'))
- tokens_grad: bfloat16 [2, 8, 256, 2048], P(None, None, 'dp', ('row', 'col'))
- attention_gain_grad: float32 [2048], P(('row', 'col', 'dp'))
- query_grad: float32 [2048, 2048], P(('row', 'dp'), 'col')
- key_grad: float32 [2048, 2048], P(('row', 'dp'), 'col')
- value_grad: float32 [2048, 2048], P(('row', 'dp'), 'col')
- output_grad: float32 [2048, 2048], P(('col', 'dp'), 'row')
- feed_gain_grad: float32 [2048], P(('row', 'col', 'dp'))
- gate_grad: float32 [2048, 8192], P(('row', 'dp'), 'col')
- up_grad: float32 [2048, 8192], P(('row', 'dp'), 'col')
- down_grad: float32 [8192, 2048], P(('col', 'dp'), 'row')
Inputs may be any that keep to these rules, and one draw needn't show every extreme that they name: `lengths`: in each micro-batch one sequence has exactly 256 tokens. `deal_order`: each row holds every number of 0 to 7 once.
All inputs are finite; a program needn't handle non-finite values.
Results may differ from a plain program's by a relative error of at most 0.023.
Values may be sent and summed in bfloat16 or wider, within the bound.
A program may use at most 256 MiB of HBM per device.

v0:
```python
import math
import jax
import jax.numpy as jnp
from jax import lax
from jax.sharding import PartitionSpec as P

D = 2048
HEADS = 32
HEAD_DIM = 64
SL = 256
MICRO = 2
EPSILON = 1e-05
ROPE_THETA = 130000.0
MASKED_SCORE = -1000000000.0


def rope_tables(slot_count, head_width):
    half_width = head_width // 2
    frequency = jnp.exp(
        jnp.arange(half_width, dtype=jnp.float32) * (-2.0 * math.log(ROPE_THETA) / head_width)
    )
    angles = jnp.arange(slot_count, dtype=jnp.float32)[:, None] * frequency[None, :]
    return (jnp.cos(angles)[:, None, :], jnp.sin(angles)[:, None, :])


def rotate(values, cosine_table, sine_table):
    half_width = values.shape[-1] // 2
    first_half = values[..., :half_width]
    second_half = values[..., half_width:]
    return jnp.concatenate(
        [
            first_half * cosine_table - second_half * sine_table,
            second_half * cosine_table + first_half * sine_table,
        ],
        axis=-1,
    )


def unrotate(grads, cosine_table, sine_table):
    half_width = grads.shape[-1] // 2
    first_half = grads[..., :half_width]
    second_half = grads[..., half_width:]
    return jnp.concatenate(
        [
            first_half * cosine_table + second_half * sine_table,
            second_half * cosine_table - first_half * sine_table,
        ],
        axis=-1,
    )


def masked_scores(queries, key_rows, length):
    positions = jnp.arange(SL, dtype=jnp.int32)
    allowed = (positions[None, :] <= positions[:, None]) & (positions[None, :] < length)
    scores = jnp.einsum(
        "qhd,khd->hqk", queries, key_rows, preferred_element_type=jnp.float32
    ) * HEAD_DIM ** (-0.5)
    return jnp.where(allowed[None], scores, MASKED_SCORE)


def attend_forward(queries, key_rows, values, length):
    scores = masked_scores(queries, key_rows, length)
    row_top = jnp.max(scores, axis=-1, keepdims=True)
    exp_scores = jnp.exp(scores - row_top)
    row_total = jnp.sum(exp_scores, axis=-1, keepdims=True)
    softmax_out = (exp_scores / row_total).astype(jnp.bfloat16)
    mixed_heads = jnp.einsum(
        "hqk,khd->qhd", softmax_out, values, preferred_element_type=jnp.float32
    )
    return (mixed_heads, row_top + jnp.log(row_total))


def attend_backward(queries, key_rows, values, length, log_total, mixed_grad):
    softmax_out = jnp.exp(masked_scores(queries, key_rows, length) - log_total)
    softmax_grad = jnp.einsum(
        "qhd,khd->hqk", mixed_grad, values, preferred_element_type=jnp.float32
    )
    values_grad = jnp.einsum(
        "hqk,qhd->khd",
        softmax_out.astype(jnp.bfloat16),
        mixed_grad,
        preferred_element_type=jnp.float32,
    )
    row_inner = jnp.sum(softmax_out * softmax_grad, axis=-1, keepdims=True)
    scores_grad = (softmax_out * (softmax_grad - row_inner)).astype(jnp.bfloat16)
    queries_grad = jnp.einsum(
        "hqk,khd->qhd", scores_grad, key_rows, preferred_element_type=jnp.float32
    ) * HEAD_DIM ** (-0.5)
    keys_grad = jnp.einsum(
        "hqk,qhd->khd", scores_grad, queries, preferred_element_type=jnp.float32
    ) * HEAD_DIM ** (-0.5)
    return (queries_grad, keys_grad, values_grad)


def column_gather(values):
    return lax.all_gather(values, "col", axis=1, tiled=True)


def row_scatter(stacked):
    return lax.psum_scatter(stacked, "row", scatter_dimension=2, tiled=True)


def row_gather(stacked):
    return lax.all_gather(stacked, "row", axis=2, tiled=True)


def column_scatter(partial_rows):
    return lax.psum_scatter(
        partial_rows.astype(jnp.bfloat16), "col", scatter_dimension=1, tiled=True
    ).astype(jnp.float32)


def feature_total(row_values):
    return lax.psum(row_values, ("row", "col"))


def norm_scale(values):
    return lax.rsqrt(feature_total(jnp.sum(values * values, axis=1)) / D + EPSILON)


def norm_backward(normed_grad, values, inverse_rms, gain_vector, upstream):
    gain_piece = jnp.sum(normed_grad * values * inverse_rms[:, None], axis=0)
    feature_dot = feature_total(jnp.sum(normed_grad * gain_vector * values, axis=1))
    result = (
        upstream
        + normed_grad * gain_vector * inverse_rms[:, None]
        - values * (inverse_rms**3 * feature_dot / D)[:, None]
    )
    return (result, gain_piece)


def per_device(
    tokens,
    lengths,
    deal_order,
    attention_gain,
    query_weight,
    key_weight,
    value_weight,
    output_weight,
    feed_gain,
    gate_weight,
    up_weight,
    down_weight,
    cotangent,
):
    head_shape = (SL, HEADS // (lax.axis_size("row") * lax.axis_size("col")), HEAD_DIM)
    dealt_rows = lax.all_to_all(
        jnp.take_along_axis(tokens, deal_order[:, :, None, None], axis=1),
        "dp",
        split_axis=1,
        concat_axis=2,
        tiled=True,
    )
    own_order = lax.dynamic_slice_in_dim(deal_order, lax.axis_index("dp"), 1, 1)
    own_lengths = jnp.take_along_axis(lengths, own_order, axis=1)[:, 0]
    cosine_table, sine_table = rope_tables(SL, HEAD_DIM)
    qkv_weights = jnp.stack((query_weight, key_weight, value_weight))
    pair_weights = jnp.stack((gate_weight, up_weight))
    qkv_grad_sum = jnp.zeros(qkv_weights.shape, jnp.float32)
    output_grad_sum = jnp.zeros(output_weight.shape, jnp.float32)
    pair_grad_sum = jnp.zeros(pair_weights.shape, jnp.float32)
    down_grad_sum = jnp.zeros(down_weight.shape, jnp.float32)
    attention_gain_sum = jnp.zeros(attention_gain.shape, jnp.float32)
    feed_gain_sum = jnp.zeros(feed_gain.shape, jnp.float32)
    row_positions = jnp.arange(SL, dtype=jnp.int32)
    output_blocks = []
    grad_blocks = []
    for micro_index in range(MICRO):
        length = own_lengths[micro_index]
        residual_in = dealt_rows[micro_index, 0].astype(jnp.float32)
        upstream = (
            cotangent[micro_index, 0].astype(jnp.float32)
            * (row_positions < length).astype(jnp.float32)[:, None]
        )
        inverse_first = norm_scale(residual_in)
        normed_first = (residual_in * inverse_first[:, None] * attention_gain).astype(jnp.bfloat16)
        normed_first_all = column_gather(normed_first)
        projected = row_scatter(
            jnp.einsum(
                "rd,kde->kre", normed_first_all, qkv_weights, preferred_element_type=jnp.float32
            )
        )
        queries = rotate(projected[0].reshape(head_shape), cosine_table, sine_table).astype(
            jnp.bfloat16
        )
        key_rows = rotate(projected[1].reshape(head_shape), cosine_table, sine_table).astype(
            jnp.bfloat16
        )
        values = projected[2].reshape(head_shape).astype(jnp.bfloat16)
        mixed_heads, log_total = attend_forward(queries, key_rows, values, length)
        mixed_all = row_gather(mixed_heads.reshape(1, SL, -1).astype(jnp.bfloat16))[0]
        middle = residual_in + column_scatter(
            jnp.dot(mixed_all, output_weight, preferred_element_type=jnp.float32)
        )
        inverse_second = norm_scale(middle)
        normed_second = (middle * inverse_second[:, None] * feed_gain).astype(jnp.bfloat16)
        normed_second_all = column_gather(normed_second)
        gate_up = row_scatter(
            jnp.einsum(
                "rd,kde->kre", normed_second_all, pair_weights, preferred_element_type=jnp.float32
            )
        )
        swish_gate = gate_up[0] / (1.0 + jnp.exp(-gate_up[0]))
        hidden = (swish_gate * gate_up[1]).astype(jnp.bfloat16)
        hidden_all = row_gather(hidden[None])[0]
        layer_rows = middle + column_scatter(
            jnp.dot(hidden_all, down_weight, preferred_element_type=jnp.float32)
        )
        output_blocks.append(layer_rows.astype(jnp.bfloat16))
        top_all = column_gather(upstream.astype(jnp.bfloat16))
        down_grad_sum = down_grad_sum + jnp.einsum(
            "rf,rd->fd", hidden_all, top_all, preferred_element_type=jnp.float32
        )
        hidden_grad = row_scatter(
            jnp.einsum("rd,fd->rf", top_all, down_weight, preferred_element_type=jnp.float32)[None]
        )[0]
        sigmoid_gate = 1.0 / (1.0 + jnp.exp(-gate_up[0]))
        gate_grad = (
            hidden_grad * gate_up[1] * sigmoid_gate * (1.0 + gate_up[0] * (1.0 - sigmoid_gate))
        )
        pair_grad_all = row_gather(
            jnp.stack((gate_grad, hidden_grad * swish_gate)).astype(jnp.bfloat16)
        )
        pair_grad_sum = pair_grad_sum + jnp.einsum(
            "rd,kre->kde", normed_second_all, pair_grad_all, preferred_element_type=jnp.float32
        )
        second_grad = column_scatter(
            jnp.einsum(
                "kre,kde->rd", pair_grad_all, pair_weights, preferred_element_type=jnp.float32
            )
        )
        middle_grad, gain_piece = norm_backward(
            second_grad, middle, inverse_second, feed_gain, upstream
        )
        feed_gain_sum = feed_gain_sum + gain_piece
        branch_all = column_gather(middle_grad.astype(jnp.bfloat16))
        output_grad_sum = output_grad_sum + jnp.einsum(
            "rh,rd->hd", mixed_all, branch_all, preferred_element_type=jnp.float32
        )
        mixed_grad = row_scatter(
            jnp.einsum("rd,hd->rh", branch_all, output_weight, preferred_element_type=jnp.float32)[
                None
            ]
        )[0]
        queries_grad, keys_grad, values_grad = attend_backward(
            queries,
            key_rows,
            values,
            length,
            log_total,
            mixed_grad.reshape(head_shape).astype(jnp.bfloat16),
        )
        turned_back = jnp.stack(
            (
                unrotate(queries_grad, cosine_table, sine_table),
                unrotate(keys_grad, cosine_table, sine_table),
                values_grad,
            )
        )
        three_all = row_gather(turned_back.reshape(3, SL, -1).astype(jnp.bfloat16))
        qkv_grad_sum = qkv_grad_sum + jnp.einsum(
            "rd,kre->kde", normed_first_all, three_all, preferred_element_type=jnp.float32
        )
        first_grad = column_scatter(
            jnp.einsum("kre,kde->rd", three_all, qkv_weights, preferred_element_type=jnp.float32)
        )
        input_grad, gain_piece = norm_backward(
            first_grad, residual_in, inverse_first, attention_gain, middle_grad
        )
        attention_gain_sum = attention_gain_sum + gain_piece
        grad_blocks.append(input_grad.astype(jnp.bfloat16))
    reduced = (
        lax.psum_scatter(
            attention_gain_sum.astype(jnp.bfloat16), "dp", scatter_dimension=0, tiled=True
        ).astype(jnp.float32),
        lax.psum_scatter(
            qkv_grad_sum[0].astype(jnp.bfloat16), "dp", scatter_dimension=0, tiled=True
        ).astype(jnp.float32),
        lax.psum_scatter(
            qkv_grad_sum[1].astype(jnp.bfloat16), "dp", scatter_dimension=0, tiled=True
        ).astype(jnp.float32),
        lax.psum_scatter(
            qkv_grad_sum[2].astype(jnp.bfloat16), "dp", scatter_dimension=0, tiled=True
        ).astype(jnp.float32),
        lax.psum_scatter(
            output_grad_sum.astype(jnp.bfloat16), "dp", scatter_dimension=0, tiled=True
        ).astype(jnp.float32),
        lax.psum_scatter(
            feed_gain_sum.astype(jnp.bfloat16), "dp", scatter_dimension=0, tiled=True
        ).astype(jnp.float32),
        lax.psum_scatter(
            pair_grad_sum[0].astype(jnp.bfloat16), "dp", scatter_dimension=0, tiled=True
        ).astype(jnp.float32),
        lax.psum_scatter(
            pair_grad_sum[1].astype(jnp.bfloat16), "dp", scatter_dimension=0, tiled=True
        ).astype(jnp.float32),
        lax.psum_scatter(
            down_grad_sum.astype(jnp.bfloat16), "dp", scatter_dimension=0, tiled=True
        ).astype(jnp.float32),
    )
    returned_out, returned_grad = (
        lax.all_to_all(
            jnp.stack(output_blocks)[:, None], "dp", split_axis=2, concat_axis=1, tiled=True
        ),
        lax.all_to_all(
            jnp.stack(grad_blocks)[:, None], "dp", split_axis=2, concat_axis=1, tiled=True
        ),
    )
    slot_of = jnp.argsort(deal_order, axis=1)[:, :, None, None]
    layer_output = jnp.take_along_axis(returned_out, slot_of, axis=1)
    tokens_grad = jnp.take_along_axis(returned_grad, slot_of, axis=1)
    return (
        layer_output,
        tokens_grad,
        reduced[0],
        reduced[1],
        reduced[2],
        reduced[3],
        reduced[4],
        reduced[5],
        reduced[6],
        reduced[7],
        reduced[8],
    )


def solution(mesh):
    in_specs = (
        P(None, None, "dp", ("row", "col")),
        P(),
        P(),
        P(("row", "col")),
        P("row", "col"),
        P("row", "col"),
        P("row", "col"),
        P("col", "row"),
        P(("row", "col")),
        P("row", "col"),
        P("row", "col"),
        P("col", "row"),
        P(None, "dp", None, ("row", "col")),
    )
    out_specs = (
        P(None, None, "dp", ("row", "col")),
        P(None, None, "dp", ("row", "col")),
        P(("row", "col", "dp")),
        P(("row", "dp"), "col"),
        P(("row", "dp"), "col"),
        P(("row", "dp"), "col"),
        P(("col", "dp"), "row"),
        P(("row", "col", "dp")),
        P(("row", "dp"), "col"),
        P(("row", "dp"), "col"),
        P(("col", "dp"), "row"),
    )
    return jax.shard_map(
        per_device, mesh=mesh, in_specs=in_specs, out_specs=out_specs, check_vma=False
    )
```

profile of v0, /device:TPU:0, one launch (start us, length us, event | category | flops | bytes accessed | tf_op | source)
XLA Modules:
  0.0 1240.4 jit_solution(1370745527233818062)
XLA Ops:
  11.4 7.3 all-to-all-start
  18.7 3.9 copy.152
  22.6 3.9 copy.153
  26.6 3.9 copy.154
  33.5 7.5 all-reduce.5
  41.7 9.3 all_gather.52
  51.8 6.3 convolution_bitcast_fusion.4
  58.2 8.5 all_gather.48
  67.5 6.4 convolution_bitcast_fusion.5
  102.4 10.7 all_gather.60
  113.9 7.9 convolution_bitcast_fusion.2
  121.8 12.0 copy.158
  133.8 12.3 copy.159
  147.9 7.0 all-reduce.4
  158.1 8.9 all_gather.54
  167.8 10.3 convolution_bitcast_fusion
  178.1 7.8 all_gather.56
  186.7 9.7 convolution_bitcast_fusion.3
  197.4 7.0 all_gather.50
  205.2 11.7 convolution_bitcast_fusion.1
  217.5 4.9 multiply_convert_fusion.2
  224.1 10.2 reduce-scatter.38.cloned.1.call-done
  234.3 4.9 multiply_convert_fusion.5
  241.6 9.2 all-gather.15.cloned.1.call-done
  250.8 10.1 fusion.24
  261.0 6.1 all-gather.11.cloned.1.call-done
  267.1 10.1 fusion.23
  277.3 3.1 all-gather.9.cloned.1.call-done
  280.4 7.2 fusion.20
  287.7 11.2 reduce-scatter.60.cloned.1.call-done
  298.9 17.5 %reduce-scatter.52.cloned.1.call-done = bf16[256,512]{1,0:T(8,128)(2,1)} async-done(((bf16[256,1024]{1,0:T(8,128)(2,1)}), bf16[256,512]{1,0:T(8,128)(2,1)}) %reduce-scatter.52.cloned.1.call-update) | async-done | bytes 262160 | tf_op jit(solution)/shard_map/reduce_scatter | solution.py:108
  318.6 7.0 all-reduce.3
  328.0 5.5 reduce-scatter.48.cloned.1.call-done
  336.2 8.7 all_gather.58
  347.5 8.1 all_gather.62
  380.5 2.7 add_convert_fusion.9
  403.6 5.3 fusion.15
  409.0 4.8 all-gather.17.cloned.1.call-done
  413.8 5.3 fusion.16
  419.1 8.0 all-gather.7.cloned.1.call-done
  427.2 7.2 fusion.17
  438.7 3.4 fusion.80
  444.0 2.7 slice_bitcast_fusion.2
  446.8 3.9 copy.216
  450.8 3.9 copy.214
  458.9 9.3 fusion.5
  468.3 11.7 add_convert_fusion.1
  481.0 15.7 %fusion.74 = f32[2,4096,1024]{2,1,0:T(8,128)} fusion(bf16[2,256,4096]{1,2,0:T(8,128)(2,1)} %all-gather.11.cloned.1.call-done, bf16[256,1024]{1,0:T(8,128)(2,1)S(1)} %copy-done.32), kind=kOutput, calls=%fused_computation.147 | convolution fusion | flops 4294967296 | bytes 38273024 | tf_op jit(solution)/shard_map/rd,kre->kde/dot_general | solution.py:225
  496.8 19.1 %fusion = bf16[2,1024,4096]{1,2,0:T(8,128)(2,1)} fusion(f32[2,4096,1024]{2,1,0:T(8,128)} %fusion.74, bf16[2,256,4096]{1,2,0:T(8,128)(2,1)S(1)} %copy-done.23, bf16[256,1024]{1,0:T(8,128)(2,1)S(1)} %copy-done.30), kind=kOutput, calls=%fused_computation.5 | convolution fusion | flops 4311744512 | bytes 55050240 | tf_op jit(solution)/shard_map/rd,kre->kde/dot_general | solution.py:225
  515.9 11.7 slice_bitcast_fusion
  527.7 11.3 copy.220
  539.0 11.6 copy.218
  552.9 7.7 all-reduce.2
  563.7 5.9 all-to-all-start.1
  572.2 21.8 %all-to-all-done.1 = bf16[2,1,256,512]{3,0,1,2:T(2,128)(2,1)S(1)} async-done(((bf16[2,1,256,512]{3,0,1,2:T(2,128)(2,1)}), bf16[2,1,256,512]{3,0,1,2:T(2,128)(2,1)S(1)}, u32[]{:S(2)}, u32[]{:S(2)}) %all-to-all-start.1) | async-done | bytes 524320 | tf_op jit(solution)/shard_map/all_to_all | solution.py:303
  594.0 3.9 all-to-all-start.2
  601.1 22.1 %all-reduce.6 = (bf16[512]{0:T(512)(128)(2,1)S(1)}, bf16[512]{0:T(512)(128)(2,1)S(1)}) all-reduce(bf16[512]{0:T(512)(128)(2,1)S(1)} %add_convert_fusion.15, bf16[512]{0:T(512)(128)(2,1)S(1)} %add_convert_fusion.14), channel_id=18, replica_groups=mesh['dp'=8,'row'=2,'col'=2] {'dp'}, use_global_device_ids=true, to_apply=%region_41.43.clone | all-reduce | flops 1024 | bytes 4096
  626.9 6.0 reduce-scatter.74.cloned.1.call-done
  635.0 68.9 %reduce-scatter.72.cloned.1.call-done = bf16[128,1024]{1,0:T(8,128)(2,1)} async-done(((bf16[1024,1024]{1,0:T(8,128)(2,1)}), bf16[128,1024]{1,0:T(8,128)(2,1)}) %reduce-scatter.72.cloned.1.call-update) | async-done | bytes 262160
  705.9 68.8 %reduce-scatter.70.cloned.1.call-done = bf16[128,1024]{1,0:T(8,128)(2,1)} async-done(((bf16[1024,1024]{1,0:T(8,128)(2,1)}), bf16[128,1024]{1,0:T(8,128)(2,1)}) %reduce-scatter.70.cloned.1.call-update) | async-done | bytes 262160
  776.7 149.5 %reduce-scatter.68.cloned.1.call-done = bf16[512,1024]{1,0:T(8,128)(2,1)} async-done(((bf16[4096,1024]{1,0:T(8,128)(2,1)}), bf16[512,1024]{1,0:T(8,128)(2,1)}) %reduce-scatter.68.cloned.1.call-update) | async-done | bytes 1048592 | tf_op jit(solution)/shard_map/reduce_scatter | solution.py:298
  926.2 2.8 convert_element_type.355
  929.0 149.4 %reduce-scatter.78.cloned.1.call-done = bf16[128,4096]{1,0:T(8,128)(2,1)} async-done(((bf16[1024,4096]{1,0:T(8,128)(2,1)}), bf16[128,4096]{1,0:T(8,128)(2,1)}) %reduce-scatter.78.cloned.1.call-update) | async-done | bytes 1048592
  1081.6 148.4 %reduce-scatter.76.cloned.1.call-done = bf16[128,4096]{1,0:T(8,128)(2,1)} async-done(((bf16[1024,4096]{1,0:T(8,128)(2,1)}), bf16[128,4096]{1,0:T(8,128)(2,1)}) %reduce-scatter.76.cloned.1.call-update) | async-done | bytes 1048592
  (370 shorter events, 145.2 us)
Async XLA Ops:
  7.2 84.0 %copy-start = (bf16[1024,1024]{1,0:T(8,128)(2,1)S(1)}, bf16[1024,1024]{1,0:T(8,128)(2,1)}, u32[]{:S(2)}) copy-start(bf16[1024,1024]{1,0:T(8,128)(2,1)} %param.22) | copy-start | bytes 6291460
  11.4 21.7 %all-to-all-start = ((bf16[2,8,32,512]{3,2,0,1:T(8,128)(2,1)}), bf16[2,8,32,512]{3,2,0,1:T(8,128)(2,1)S(1)}, u32[]{:S(2)}, u32[]{:S(2)}) async-start(bf16[2,8,32,512]{3,2,0,1:T(8,128)(2,1)} %copy.151), calls=%async_computation | async-start | bytes 1048576 | tf_op jit(solution)/shard_map/all_to_all | solution.py:148
  18.6 62.7 %reduce-scatter.42.cloned.1.call-start = ((), (), s32[]{:S(2)}) async-start(), calls=%async_computation.31 | async-start | bytes 4718592 | tf_op jit(solution)/shard_map/reduce_scatter | solution.py:100
  26.6 15.0 %copy-start.63 = (f32[512]{0:T(512)S(1)}, f32[512]{0:T(512)}, u32[]{:S(2)}) copy-start(f32[512]{0:T(512)} %param.18) | copy-start | bytes 6148
  41.0 10.1 copy-start.73
  41.0 10.1 copy-start.75
  58.2 25.3 %reduce-scatter.34.cloned.1.call-start = ((), (), s32[]{:S(2)}) async-start(), calls=%async_computation.26 | async-start | bytes 4718592 | tf_op jit(solution)/shard_map/reduce_scatter | solution.py:100
  73.9 72.2 %reduce-scatter.36.cloned.1.call-start = ((), (), s32[]{:S(2)}) async-start(), calls=%async_computation.27 | async-start | bytes 786432 | tf_op jit(solution)/shard_map/reduce_scatter | solution.py:108
  79.0 22.1 %copy-start.69 = (f32[256]{0:T(256)}, f32[256]{0:T(256)S(1)}, u32[]{:S(2)}) copy-start(f32[256]{0:T(256)S(1)} %get-tuple-element.152) | copy-start | bytes 3076
  79.0 22.1 %copy-start.71 = (f32[256]{0:T(256)}, f32[256]{0:T(256)S(1)}, u32[]{:S(2)}) copy-start(f32[256]{0:T(256)S(1)} %get-tuple-element.153) | copy-start | bytes 3076
  85.9 6.9 copy-start.42
  92.7 53.4 %reduce-scatter.44.cloned.1.call-start = ((), (), s32[]{:S(2)}) async-start(), calls=%async_computation.32 | async-start | bytes 786432 | tf_op jit(solution)/shard_map/reduce_scatter | solution.py:108
  101.1 116.4 %reduce-scatter.58.cloned.1.call-start = ((), (), s32[]{:S(2)}) async-start(), calls=%async_computation.42 | async-start | bytes 6291456 | tf_op jit(solution)/shard_map/reduce_scatter | solution.py:100
  121.8 95.7 %reduce-scatter.46.cloned.1.call-start = ((), (), s32[]{:S(2)}) async-start(), calls=%async_computation.33 | async-start | bytes 12582912 | tf_op jit(solution)/shard_map/reduce_scatter | solution.py:100
  133.8 22.4 %copy-start.59 = (f32[512]{0:T(512)S(1)}, f32[512]{0:T(512)}, u32[]{:S(2)}) copy-start(f32[512]{0:T(512)} %param.23) | copy-start | bytes 6148
  156.2 10.8 copy-start.65
  178.1 46.0 %reduce-scatter.50.cloned.1.call-start = ((), (), s32[]{:S(2)}) async-start(), calls=%async_computation.36 | async-start | bytes 6291456 | tf_op jit(solution)/shard_map/reduce_scatter | solution.py:100
  196.5 37.8 %reduce-scatter.38.cloned.1.call-start = ((), (), s32[]{:S(2)}) async-start(), calls=%async_computation.28 | async-start | bytes 12582912 | tf_op jit(solution)/shard_map/reduce_scatter | solution.py:100
  217.0 33.8 %all-gather.15.cloned.1.call-start = ((), (), s32[]{:S(2)}) async-start(), calls=%async_computation.43 | async-start | bytes 6291456 | tf_op jit(solution)/shard_map/all_gather | solution.py:104
  224.0 43.1 %all-gather.11.cloned.1.call-start = ((), (), s32[]{:S(2)}) async-start(), calls=%async_computation.37 | async-start | bytes 6291456 | tf_op jit(solution)/shard_map/all_gather | solution.py:104
  240.8 39.6 %all-gather.9.cloned.1.call-start = ((), (), s32[]{:S(2)}) async-start(), calls=%async_computation.34 | async-start | bytes 3145728 | tf_op jit(solution)/shard_map/all_gather | solution.py:104
  241.5 57.3 %reduce-scatter.60.cloned.1.call-start = ((), (), s32[]{:S(2)}) async-start(), calls=%async_computation.44 | async-start | bytes 786432 | tf_op jit(solution)/shard_map/reduce_scatter | solution.py:108
  261.0 55.4 %reduce-scatter.52.cloned.1.call-start = ((), (), s32[]{:S(2)}) async-start(), calls=%async_computation.38 | async-start | bytes 786432 | tf_op jit(solution)/shard_map/reduce_scatter | solution.py:108
  277.2 39.1 %copy-start.10 = (bf16[256,512]{1,0:T(8,128)(2,1)S(1)}, bf16[256,512]{1,0:T(8,128)(2,1)}, u32[]{:S(2)}) copy-start(bf16[256,512]{1,0:T(8,128)(2,1)} %reduce-scatter.44.cloned.1.call-done) | copy-start | bytes 786436
  277.2 56.3 %reduce-scatter.48.cloned.1.call-start = ((), (), s32[]{:S(2)}) async-start(), calls=%async_computation.35 | async-start | bytes 786432 | tf_op jit(solution)/shard_map/reduce_scatter | solution.py:108
  287.6 72.9 %reduce-scatter.54.cloned.1.call-start = ((), (), s32[]{:S(2)}) async-start(), calls=%async_computation.39 | async-start | bytes 1572864 | tf_op jit(solution)/shard_map/reduce_scatter | solution.py:100
  347.4 22.8 %reduce-scatter.62.cloned.1.call-start = ((), (), s32[]{:S(2)}) async-start(), calls=%async_computation.45 | async-start | bytes 1572864 | tf_op jit(solution)/shard_map/reduce_scatter | solution.py:100
  358.1 45.5 %all-gather.13.cloned.1.call-start = ((), (), s32[]{:S(2)}) async-start(), calls=%async_computation.40 | async-start | bytes 2359296 | tf_op jit(solution)/shard_map/all_gather | solution.py:104
  391.3 22.5 %all-gather.17.cloned.1.call-start = ((), (), s32[]{:S(2)}) async-start(), calls=%async_computation.46 | async-start | bytes 2359296 | tf_op jit(solution)/shard_map/all_gather | solution.py:104
  402.8 24.4 %all-gather.7.cloned.1.call-start = ((), (), s32[]{:S(2)}) async-start(), calls=%async_computation.29 | async-start | bytes 3145728 | tf_op jit(solution)/shard_map/all_gather | solution.py:104
  403.6 147.2 %reduce-scatter.56.cloned.1.call-start = ((), (), s32[]{:S(2)}) async-start(), calls=%async_computation.41 | async-start | bytes 786432 | tf_op jit(solution)/shard_map/reduce_scatter | solution.py:108
  408.9 141.8 %reduce-scatter.64.cloned.1.call-start = ((), (), s32[]{:S(2)}) async-start(), calls=%async_computation.47 | async-start | bytes 786432 | tf_op jit(solution)/shard_map/reduce_scatter | solution.py:108
  419.1 15.6 %copy-start.21 = (bf16[256,1024]{1,0:T(8,128)(2,1)S(1)}, bf16[256,1024]{1,0:T(8,128)(2,1)}, u32[]{:S(2)}) copy-start(bf16[256,1024]{1,0:T(8,128)(2,1)} %copy-done.20) | copy-start | bytes 1572868
  419.1 141.5 %reduce-scatter.40.cloned.1.call-start = ((), (), s32[]{:S(2)}) async-start(), calls=%async_computation.30 | async-start | bytes 786432 | tf_op jit(solution)/shard_map/reduce_scatter | solution.py:108
  434.4 164.9 %reduce-scatter.66.cloned.1.call-start = ((), (), s32[]{:S(2)}) async-start(), calls=%async_computation.48 | async-start | bytes 2359296 | tf_op jit(solution)/shard_map/reduce_scatter | solution.py:286
  437.7 195.2 %reduce-scatter.74.cloned.1.call-start = ((), (), s32[]{:S(2)}) async-start(), calls=%async_computation.52 | async-start | bytes 2359296
  450.7 253.1 %reduce-scatter.72.cloned.1.call-start = ((), (), s32[]{:S(2)}) async-start(), calls=%async_computation.51 | async-start | bytes 2359296
  454.7 319.9 %reduce-scatter.70.cloned.1.call-start = ((), (), s32[]{:S(2)}) async-start(), calls=%async_computation.50 | async-start | bytes 2359296
  457.4 10.9 copy-start.18
  457.4 468.8 %reduce-scatter.68.cloned.1.call-start = ((), (), s32[]{:S(2)}) async-start(), calls=%async_computation.49 | async-start | bytes 9437184 | tf_op jit(solution)/shard_map/reduce_scatter | solution.py:298
  458.9 9.3 copy-start.9
  480.0 16.8 %copy-start.30 = (bf16[256,1024]{1,0:T(8,128)(2,1)S(1)}, bf16[256,1024]{1,0:T(8,128)(2,1)}, u32[]{:S(2)}) copy-start(bf16[256,1024]{1,0:T(8,128)(2,1)} %copy-done.29) | copy-start | bytes 1572868
  480.0 598.4 %reduce-scatter.78.cloned.1.call-start = ((), (), s32[]{:S(2)}) async-start(), calls=%async_computation.54 | async-start | bytes 9437184
  481.0 15.7 %copy-start.23 = (bf16[2,256,4096]{1,2,0:T(8,128)(2,1)S(1)}, bf16[2,256,4096]{1,2,0:T(8,128)(2,1)}, u32[]{:S(2)}) copy-start(bf16[2,256,4096]{1,2,0:T(8,128)(2,1)} %all-gather.15.cloned.1.call-done) | copy-start | bytes 12582916
  539.0 691.1 %reduce-scatter.76.cloned.1.call-start = ((), (), s32[]{:S(2)}) async-start(), calls=%async_computation.53 | async-start | bytes 9437184
  550.6 10.0 copy-start.84
  550.6 10.0 copy-start.11
  550.6 10.0 copy-start.22
  550.6 10.0 copy-start.26
  550.6 10.0 copy-start.70
  550.6 10.0 copy-start.77
  550.7 11.6 copy-start.39
  562.2 7.3 copy-start.68
  562.2 8.1 copy-start.82
  562.2 8.1 copy-start.25
  562.3 8.1 copy-start.41
  562.3 8.1 copy-start.66
  562.3 8.1 copy-start.72
  562.3 8.1 copy-start.78
  563.7 30.3 %all-to-all-start.1 = ((bf16[2,1,256,512]{3,0,1,2:T(2,128)(2,1)}), bf16[2,1,256,512]{3,0,1,2:T(2,128)(2,1)S(1)}, u32[]{:S(2)}, u32[]{:S(2)}) async-start(bf16[2,1,256,512]{3,0,1,2:T(2,128)(2,1)} %copy.161), calls=%async_computation.9 | async-start | bytes 1048576 | tf_op jit(solution)/shard_map/all_to_all | solution.py:303
  570.4 27.6 %copy-start.85 = (u32[32]{0:T(128)S(1)}, u32[32]{0:T(128)}, u32[]{:S(2)}) copy-start(u32[32]{0:T(128)} %constant.126) | copy-start | bytes 388
  570.5 28.8 %copy-start.79 = (f32[512]{0:T(512)S(1)}, f32[512]{0:T(512)}, u32[]{:S(2)}) copy-start(f32[512]{0:T(512)} %get-tuple-element.60) | copy-start | bytes 6148
  570.5 28.8 %copy-start.80 = (f32[512]{0:T(512)S(1)}, f32[512]{0:T(512)}, u32[]{:S(2)}) copy-start(f32[512]{0:T(512)} %get-tuple-element.69) | copy-start | bytes 6148
  594.0 31.0 %all-to-all-start.2 = ((bf16[2,1,256,512]{3,0,1,2:T(2,128)(2,1)}), bf16[2,1,256,512]{3,0,1,2:T(2,128)(2,1)S(1)}, u32[]{:S(2)}, u32[]{:S(2)}) async-start(bf16[2,1,256,512]{3,0,1,2:T(2,128)(2,1)} %copy.185), calls=%async_computation.18 | async-start | bytes 1048576 | tf_op jit(solution)/shard_map/all_to_all | solution.py:306
  (54 other events, 89.3 us)
Sparse Core Ops, SparseCore 0:
  58.3 9.0 reduce-scatter.41
  74.0 9.3 reduce-scatter.33
  92.8 16.9 reduce-scatter.35
  112.6 14.3 reduce-scatter.43
  129.1 12.0 reduce-scatter.57
  178.2 17.2 reduce-scatter.45
  197.9 13.2 reduce-scatter.49
  217.1 17.1 reduce-scatter.37
  235.8 14.9 all-gather.14
  252.2 14.8 all-gather.10
  268.6 11.7 all-gather.8
  283.1 15.7 reduce-scatter.59
  301.8 14.5 reduce-scatter.51
  319.0 14.5 reduce-scatter.47
  347.5 8.5 reduce-scatter.53
  358.2 9.6 reduce-scatter.61
  391.4 9.8 all-gather.12
  402.9 10.8 all-gather.16
  415.4 11.7 all-gather.6
  429.9 15.7 reduce-scatter.55
  448.5 14.5 reduce-scatter.63
  466.0 14.5 reduce-scatter.39
  484.1 67.7 reduce-scatter.65
  555.3 77.5 reduce-scatter.73
  637.0 66.7 reduce-scatter.71
  707.8 66.8 reduce-scatter.69
  778.2 148.0 reduce-scatter.67
  930.3 148.0 reduce-scatter.77
  1082.0 147.9 reduce-scatter.75
where the time goes:
time: 1250 us; the launch traced here: 1240 us
  waiting for transfers between devices  693 us (55%)
  matrix products  182 us (15%)
  local copies, waits for them, and re-layouts  140 us (11%)
  blocking collectives  125 us (10%)
  other arithmetic  65.1 us (5%)
  starting transfers between devices  19.2 us (2%)
  between operations  16.4 us (1%)
    unnamed x34, waiting for transfers between devices  443 us
    reduce_scatter x1, waiting for transfers between devices, per_device(): lax.psum_scatter(down_grad_sum.astype(jnp.bfloat16), 'dp', scatter_dimens...  149 us
    unnamed x195, local copies, waits for them, and re-layouts  97.5 us
    all_gather x8, blocking collectives, column_gather(): return lax.all_gather(values, 'col', axis=1, tiled=True)  69 us
    dot_general x2, matrix products, per_device(): jnp.einsum('rd,kre->kde', normed_second_all, pair_grad_all, preferred_ele...  34.9 us
    reduce_scatter x8, waiting for transfers between devices, column_scatter(): lax.psum_scatter(partial_rows.astype(jnp.bfloat16), 'col', scatter_dimens...  34.2 us
    all_gather x6, waiting for transfers between devices, row_gather(): return lax.all_gather(stacked, 'row', axis=2, tiled=True)  31.3 us
    psum x4, blocking collectives, feature_total(): return lax.psum(row_values, ('row', 'col'))  29.1 us
  transfers between devices with their start and end apart: 32, of which 17 were waited for; matrix products, arithmetic and copies ran while one was open for 26% of the time, Pallas kernels for 0%

commit v1 on v0

--- a/solution.py
+++ b/solution.py
@@ -111,7 +111,8 @@
 
 
 def feature_total(row_values):
-    return lax.psum(row_values, ("row", "col"))
+    state_groups_on = lambda w_in: lax.psum(lax.psum(w_in, "col"), "row")
+    return state_groups_on(row_values)
 
 
 def norm_scale(values):

time: 1250 us -> 1250 us (level)
    psum x4 -> x8, blocking collectives: 29.1 us -> 32.2 us  [feature_total(): state_groups_on = lambda w_in: lax.psum(lax.psum(w_in, 'col'), 'row')]
  transfers between devices with their start and end apart: 32 -> 32, of which waited for: 17 -> 18; matrix products, arithmetic and copies ran while one was open for 26% -> 26% of each run, Pallas kernels for 0% -> 0%
where the time goes in v1:
time: 1250 us; the launch traced here: 1240 us
  waiting for transfers between devices  691 us (55%)
  matrix products  182 us (15%)
  local copies, waits for them, and re-layouts  140 us (11%)
  blocking collectives  128 us (10%)
  other arithmetic  65.1 us (5%)
  starting transfers between devices  19.5 us (2%)
  between operations  16.3 us (1%)
    unnamed x34, waiting for transfers between devices  443 us
    reduce_scatter x1, waiting for transfers between devices, per_device(): lax.psum_scatter(down_grad_sum.astype(jnp.bfloat16), 'dp', scatter_dimens...  149 us
    unnamed x195, local copies, waits for them, and re-layouts  97.8 us
    all_gather x8, blocking collectives, column_gather(): return lax.all_gather(values, 'col', axis=1, tiled=True)  69.4 us
    dot_general x2, matrix products, per_device(): jnp.einsum('rd,kre->kde', normed_second_all, pair_grad_all, preferred_ele...  34.9 us
    reduce_scatter x8, waiting for transfers between devices, column_scatter(): lax.psum_scatter(partial_rows.astype(jnp.bfloat16), 'col', scatter_dimens...  32.5 us
    psum x8, blocking collectives, feature_total(): state_groups_on = lambda w_in: lax.psum(lax.psum(w_in, 'col'), 'row')  32.2 us
    all_gather x6, waiting for transfers between devices, row_gather(): return lax.all_gather(stacked, 'row', axis=2, tiled=True)  31.2 us
  transfers between devices with their start and end apart: 32, of which 18 were waited for; matrix products, arithmetic and copies ran while one was open for 26% of the time, Pallas kernels for 0%

profile of v1, /device:TPU:0, one launch (start us, length us, event | category | flops | bytes accessed | tf_op | source)
XLA Modules:
  0.0 1242.6 jit_solution(2050697084924025736)
XLA Ops:
  11.4 7.3 all-to-all-start
  18.7 3.9 copy.152
  22.6 3.9 copy.153
  26.6 3.9 copy.154
  33.5 4.9 all-reduce.5
  41.6 9.1 all_gather.52
  51.5 6.3 convolution_bitcast_fusion.4
  57.9 8.2 all_gather.48
  66.9 6.5 convolution_bitcast_fusion.5
  102.8 10.8 all_gather.60
  114.3 7.8 convolution_bitcast_fusion.2
  122.2 12.0 copy.158
  134.2 12.3 copy.159
  148.4 5.6 all-reduce.4
  154.0 3.1 all-reduce.8
  160.4 9.0 all_gather.54
  170.2 10.2 convolution_bitcast_fusion
  180.5 8.2 all_gather.56
  189.5 9.6 convolution_bitcast_fusion.3
  200.1 7.3 all_gather.50
  208.1 11.6 convolution_bitcast_fusion.1
  220.3 4.9 multiply_convert_fusion.2
  226.8 9.8 reduce-scatter.38.cloned.1.call-done
  236.6 4.9 multiply_convert_fusion.5
  243.8 9.2 all-gather.15.cloned.1.call-done
  253.1 10.1 fusion.24
  263.3 6.1 all-gather.11.cloned.1.call-done
  269.4 10.1 fusion.23
  279.5 3.1 all-gather.9.cloned.1.call-done
  282.7 7.2 fusion.20
  289.9 11.2 reduce-scatter.60.cloned.1.call-done
  301.1 17.5 %reduce-scatter.52.cloned.1.call-done = bf16[256,512]{1,0:T(8,128)(2,1)} async-done(((bf16[256,1024]{1,0:T(8,128)(2,1)}), bf16[256,512]{1,0:T(8,128)(2,1)}) %reduce-scatter.52.cloned.1.call-update) | async-done | bytes 262160 | tf_op jit(solution)/shard_map/reduce_scatter | solution.py:108
  320.8 5.6 all-reduce.3
  326.4 3.1 all-reduce.7
  332.1 3.8 reduce-scatter.48.cloned.1.call-done
  338.5 8.7 all_gather.58
  349.8 8.1 all_gather.62
  406.0 5.3 fusion.15
  411.3 4.7 all-gather.17.cloned.1.call-done
  416.0 5.3 fusion.16
  421.4 8.0 all-gather.7.cloned.1.call-done
  429.4 7.2 fusion.17
  441.0 3.4 fusion.80
  449.0 3.9 copy.216
  453.0 3.9 copy.214
  461.2 9.3 fusion.5
  470.5 11.7 add_convert_fusion.1
  483.2 15.7 %fusion.74 = f32[2,4096,1024]{2,1,0:T(8,128)} fusion(bf16[2,256,4096]{1,2,0:T(8,128)(2,1)} %all-gather.11.cloned.1.call-done, bf16[256,1024]{1,0:T(8,128)(2,1)S(1)} %copy-done.32), kind=kOutput, calls=%fused_computation.147 | convolution fusion | flops 4294967296 | bytes 38273024 | tf_op jit(solution)/shard_map/rd,kre->kde/dot_general | solution.py:226
  499.0 19.1 %fusion = bf16[2,1024,4096]{1,2,0:T(8,128)(2,1)} fusion(f32[2,4096,1024]{2,1,0:T(8,128)} %fusion.74, bf16[2,256,4096]{1,2,0:T(8,128)(2,1)S(1)} %copy-done.23, bf16[256,1024]{1,0:T(8,128)(2,1)S(1)} %copy-done.30), kind=kOutput, calls=%fused_computation.5 | convolution fusion | flops 4311744512 | bytes 55050240 | tf_op jit(solution)/shard_map/rd,kre->kde/dot_general | solution.py:226
  518.1 11.8 slice_bitcast_fusion
  529.9 11.3 copy.220
  541.3 11.8 copy.218
  555.3 4.9 all-reduce.2
  565.8 6.0 all-to-all-start.1
  574.5 21.7 %all-to-all-done.1 = bf16[2,1,256,512]{3,0,1,2:T(2,128)(2,1)S(1)} async-done(((bf16[2,1,256,512]{3,0,1,2:T(2,128)(2,1)}), bf16[2,1,256,512]{3,0,1,2:T(2,128)(2,1)S(1)}, u32[]{:S(2)}, u32[]{:S(2)}) %all-to-all-start.1) | async-done | bytes 524320 | tf_op jit(solution)/shard_map/all_to_all | solution.py:304
  596.2 4.0 all-to-all-start.2
  603.4 22.1 %all-reduce.10 = (bf16[512]{0:T(512)(128)(2,1)S(1)}, bf16[512]{0:T(512)(128)(2,1)S(1)}) all-reduce(bf16[512]{0:T(512)(128)(2,1)S(1)} %add_convert_fusion.15, bf16[512]{0:T(512)(128)(2,1)S(1)} %add_convert_fusion.14), channel_id=18, replica_groups=mesh['dp'=8,'row'=2,'col'=2] {'dp'}, use_global_device_ids=true, to_apply=%region_49.51.clone | all-reduce | flops 1024 | bytes 4096
  629.1 6.2 reduce-scatter.74.cloned.1.call-done
  637.4 68.8 %reduce-scatter.72.cloned.1.call-done = bf16[128,1024]{1,0:T(8,128)(2,1)} async-done(((bf16[1024,1024]{1,0:T(8,128)(2,1)}), bf16[128,1024]{1,0:T(8,128)(2,1)}) %reduce-scatter.72.cloned.1.call-update) | async-done | bytes 262160
  708.2 68.8 %reduce-scatter.70.cloned.1.call-done = bf16[128,1024]{1,0:T(8,128)(2,1)} async-done(((bf16[1024,1024]{1,0:T(8,128)(2,1)}), bf16[128,1024]{1,0:T(8,128)(2,1)}) %reduce-scatter.70.cloned.1.call-update) | async-done | bytes 262160
  779.0 149.4 %reduce-scatter.68.cloned.1.call-done = bf16[512,1024]{1,0:T(8,128)(2,1)} async-done(((bf16[4096,1024]{1,0:T(8,128)(2,1)}), bf16[512,1024]{1,0:T(8,128)(2,1)}) %reduce-scatter.68.cloned.1.call-update) | async-done | bytes 1048592 | tf_op jit(solution)/shard_map/reduce_scatter | solution.py:299
  928.5 2.8 convert_element_type.355
  931.3 149.3 %reduce-scatter.78.cloned.1.call-done = bf16[128,4096]{1,0:T(8,128)(2,1)} async-done(((bf16[1024,4096]{1,0:T(8,128)(2,1)}), bf16[128,4096]{1,0:T(8,128)(2,1)}) %reduce-scatter.78.cloned.1.call-update) | async-done | bytes 1048592
  1083.8 148.4 %reduce-scatter.76.cloned.1.call-done = bf16[128,4096]{1,0:T(8,128)(2,1)} async-done(((bf16[1024,4096]{1,0:T(8,128)(2,1)}), bf16[128,4096]{1,0:T(8,128)(2,1)}) %reduce-scatter.76.cloned.1.call-update) | async-done | bytes 1048592
  (374 shorter events, 156.2 us)
Async XLA Ops:
  7.2 84.3 %copy-start = (bf16[1024,1024]{1,0:T(8,128)(2,1)S(1)}, bf16[1024,1024]{1,0:T(8,128)(2,1)}, u32[]{:S(2)}) copy-start(bf16[1024,1024]{1,0:T(8,128)(2,1)} %param.22) | copy-start | bytes 6291460
  11.4 21.7 %all-to-all-start = ((bf16[2,8,32,512]{3,2,0,1:T(8,128)(2,1)}), bf16[2,8,32,512]{3,2,0,1:T(8,128)(2,1)S(1)}, u32[]{:S(2)}, u32[]{:S(2)}) async-start(bf16[2,8,32,512]{3,2,0,1:T(8,128)(2,1)} %copy.151), calls=%async_computation | async-start | bytes 1048576 | tf_op jit(solution)/shard_map/all_to_all | solution.py:149
  18.6 62.2 %reduce-scatter.42.cloned.1.call-start = ((), (), s32[]{:S(2)}) async-start(), calls=%async_computation.31 | async-start | bytes 4718592 | tf_op jit(solution)/shard_map/reduce_scatter | solution.py:100
  26.6 14.8 %copy-start.63 = (f32[512]{0:T(512)S(1)}, f32[512]{0:T(512)}, u32[]{:S(2)}) copy-start(f32[512]{0:T(512)} %param.18) | copy-start | bytes 6148
  40.8 9.8 copy-start.73
  40.9 9.8 copy-start.75
  57.8 26.0 %reduce-scatter.34.cloned.1.call-start = ((), (), s32[]{:S(2)}) async-start(), calls=%async_computation.26 | async-start | bytes 4718592 | tf_op jit(solution)/shard_map/reduce_scatter | solution.py:100
  73.4 73.1 %reduce-scatter.36.cloned.1.call-start = ((), (), s32[]{:S(2)}) async-start(), calls=%async_computation.27 | async-start | bytes 786432 | tf_op jit(solution)/shard_map/reduce_scatter | solution.py:108
  78.5 23.0 %copy-start.69 = (f32[256]{0:T(256)}, f32[256]{0:T(256)S(1)}, u32[]{:S(2)}) copy-start(f32[256]{0:T(256)S(1)} %get-tuple-element.160) | copy-start | bytes 3076
  78.6 23.0 %copy-start.71 = (f32[256]{0:T(256)}, f32[256]{0:T(256)S(1)}, u32[]{:S(2)}) copy-start(f32[256]{0:T(256)S(1)} %get-tuple-element.161) | copy-start | bytes 3076
  86.2 6.9 copy-start.42
  93.0 53.5 %reduce-scatter.44.cloned.1.call-start = ((), (), s32[]{:S(2)}) async-start(), calls=%async_computation.32 | async-start | bytes 786432 | tf_op jit(solution)/shard_map/reduce_scatter | solution.py:108
  101.5 118.8 %reduce-scatter.58.cloned.1.call-start = ((), (), s32[]{:S(2)}) async-start(), calls=%async_computation.42 | async-start | bytes 6291456 | tf_op jit(solution)/shard_map/reduce_scatter | solution.py:100
  122.2 98.1 %reduce-scatter.46.cloned.1.call-start = ((), (), s32[]{:S(2)}) async-start(), calls=%async_computation.33 | async-start | bytes 12582912 | tf_op jit(solution)/shard_map/reduce_scatter | solution.py:100
  134.2 24.2 %copy-start.59 = (f32[512]{0:T(512)S(1)}, f32[512]{0:T(512)}, u32[]{:S(2)}) copy-start(f32[512]{0:T(512)} %param.23) | copy-start | bytes 6148
  158.5 10.9 copy-start.65
  180.4 46.4 %reduce-scatter.50.cloned.1.call-start = ((), (), s32[]{:S(2)}) async-start(), calls=%async_computation.36 | async-start | bytes 6291456 | tf_op jit(solution)/shard_map/reduce_scatter | solution.py:100
  199.2 37.4 %reduce-scatter.38.cloned.1.call-start = ((), (), s32[]{:S(2)}) async-start(), calls=%async_computation.28 | async-start | bytes 12582912 | tf_op jit(solution)/shard_map/reduce_scatter | solution.py:100
  219.8 33.3 %all-gather.15.cloned.1.call-start = ((), (), s32[]{:S(2)}) async-start(), calls=%async_computation.43 | async-start | bytes 6291456 | tf_op jit(solution)/shard_map/all_gather | solution.py:104
  226.7 42.6 %all-gather.11.cloned.1.call-start = ((), (), s32[]{:S(2)}) async-start(), calls=%async_computation.37 | async-start | bytes 6291456 | tf_op jit(solution)/shard_map/all_gather | solution.py:104
  243.1 39.6 %all-gather.9.cloned.1.call-start = ((), (), s32[]{:S(2)}) async-start(), calls=%async_computation.34 | async-start | bytes 3145728 | tf_op jit(solution)/shard_map/all_gather | solution.py:104
  243.8 57.3 %reduce-scatter.60.cloned.1.call-start = ((), (), s32[]{:S(2)}) async-start(), calls=%async_computation.44 | async-start | bytes 786432 | tf_op jit(solution)/shard_map/reduce_scatter | solution.py:108
  263.2 55.4 %reduce-scatter.52.cloned.1.call-start = ((), (), s32[]{:S(2)}) async-start(), calls=%async_computation.38 | async-start | bytes 786432 | tf_op jit(solution)/shard_map/reduce_scatter | solution.py:108
  279.5 39.1 %copy-start.10 = (bf16[256,512]{1,0:T(8,128)(2,1)S(1)}, bf16[256,512]{1,0:T(8,128)(2,1)}, u32[]{:S(2)}) copy-start(bf16[256,512]{1,0:T(8,128)(2,1)} %reduce-scatter.44.cloned.1.call-done) | copy-start | bytes 786436
  279.5 56.3 %reduce-scatter.48.cloned.1.call-start = ((), (), s32[]{:S(2)}) async-start(), calls=%async_computation.35 | async-start | bytes 786432 | tf_op jit(solution)/shard_map/reduce_scatter | solution.py:108
  289.9 72.9 %reduce-scatter.54.cloned.1.call-start = ((), (), s32[]{:S(2)}) async-start(), calls=%async_computation.39 | async-start | bytes 1572864 | tf_op jit(solution)/shard_map/reduce_scatter | solution.py:100
  349.7 22.8 %reduce-scatter.62.cloned.1.call-start = ((), (), s32[]{:S(2)}) async-start(), calls=%async_computation.45 | async-start | bytes 1572864 | tf_op jit(solution)/shard_map/reduce_scatter | solution.py:100
  360.4 45.5 %all-gather.13.cloned.1.call-start = ((), (), s32[]{:S(2)}) async-start(), calls=%async_computation.40 | async-start | bytes 2359296 | tf_op jit(solution)/shard_map/all_gather | solution.py:104
  393.6 22.4 %all-gather.17.cloned.1.call-start = ((), (), s32[]{:S(2)}) async-start(), calls=%async_computation.46 | async-start | bytes 2359296 | tf_op jit(solution)/shard_map/all_gather | solution.py:104
  405.1 24.3 %all-gather.7.cloned.1.call-start = ((), (), s32[]{:S(2)}) async-start(), calls=%async_computation.29 | async-start | bytes 3145728 | tf_op jit(solution)/shard_map/all_gather | solution.py:104
  405.9 147.3 %reduce-scatter.56.cloned.1.call-start = ((), (), s32[]{:S(2)}) async-start(), calls=%async_computation.41 | async-start | bytes 786432 | tf_op jit(solution)/shard_map/reduce_scatter | solution.py:108
  411.3 142.0 %reduce-scatter.64.cloned.1.call-start = ((), (), s32[]{:S(2)}) async-start(), calls=%async_computation.47 | async-start | bytes 786432 | tf_op jit(solution)/shard_map/reduce_scatter | solution.py:108
  421.3 15.6 %copy-start.21 = (bf16[256,1024]{1,0:T(8,128)(2,1)S(1)}, bf16[256,1024]{1,0:T(8,128)(2,1)}, u32[]{:S(2)}) copy-start(bf16[256,1024]{1,0:T(8,128)(2,1)} %copy-done.20) | copy-start | bytes 1572868
  421.3 141.4 %reduce-scatter.40.cloned.1.call-start = ((), (), s32[]{:S(2)}) async-start(), calls=%async_computation.30 | async-start | bytes 786432 | tf_op jit(solution)/shard_map/reduce_scatter | solution.py:108
  436.6 164.9 %reduce-scatter.66.cloned.1.call-start = ((), (), s32[]{:S(2)}) async-start(), calls=%async_computation.48 | async-start | bytes 2359296 | tf_op jit(solution)/shard_map/reduce_scatter | solution.py:287
  440.0 195.3 %reduce-scatter.74.cloned.1.call-start = ((), (), s32[]{:S(2)}) async-start(), calls=%async_computation.52 | async-start | bytes 2359296
  453.0 253.2 %reduce-scatter.72.cloned.1.call-start = ((), (), s32[]{:S(2)}) async-start(), calls=%async_computation.51 | async-start | bytes 2359296
  457.0 320.0 %reduce-scatter.70.cloned.1.call-start = ((), (), s32[]{:S(2)}) async-start(), calls=%async_computation.50 | async-start | bytes 2359296
  459.6 10.9 copy-start.18
  459.6 468.8 %reduce-scatter.68.cloned.1.call-start = ((), (), s32[]{:S(2)}) async-start(), calls=%async_computation.49 | async-start | bytes 9437184 | tf_op jit(solution)/shard_map/reduce_scatter | solution.py:299
  461.2 9.3 copy-start.9
  482.2 16.8 %copy-start.30 = (bf16[256,1024]{1,0:T(8,128)(2,1)S(1)}, bf16[256,1024]{1,0:T(8,128)(2,1)}, u32[]{:S(2)}) copy-start(bf16[256,1024]{1,0:T(8,128)(2,1)} %copy-done.29) | copy-start | bytes 1572868
  482.2 598.4 %reduce-scatter.78.cloned.1.call-start = ((), (), s32[]{:S(2)}) async-start(), calls=%async_computation.54 | async-start | bytes 9437184
  483.2 15.7 %copy-start.23 = (bf16[2,256,4096]{1,2,0:T(8,128)(2,1)S(1)}, bf16[2,256,4096]{1,2,0:T(8,128)(2,1)}, u32[]{:S(2)}) copy-start(bf16[2,256,4096]{1,2,0:T(8,128)(2,1)} %all-gather.15.cloned.1.call-done) | copy-start | bytes 12582916
  541.2 691.1 %reduce-scatter.76.cloned.1.call-start = ((), (), s32[]{:S(2)}) async-start(), calls=%async_computation.53 | async-start | bytes 9437184
  553.1 9.6 copy-start.84
  553.1 9.7 copy-start.11
  553.1 9.7 copy-start.22
  553.1 9.7 copy-start.26
  553.1 9.7 copy-start.70
  553.1 9.7 copy-start.77
  553.2 11.2 copy-start.39
  564.3 7.5 copy-start.68
  564.4 8.3 copy-start.82
  564.4 8.3 copy-start.25
  564.4 8.3 copy-start.41
  564.4 8.3 copy-start.66
  564.4 8.3 copy-start.72
  564.4 8.3 copy-start.78
  565.8 30.4 %all-to-all-start.1 = ((bf16[2,1,256,512]{3,0,1,2:T(2,128)(2,1)}), bf16[2,1,256,512]{3,0,1,2:T(2,128)(2,1)S(1)}, u32[]{:S(2)}, u32[]{:S(2)}) async-start(bf16[2,1,256,512]{3,0,1,2:T(2,128)(2,1)} %copy.161), calls=%async_computation.9 | async-start | bytes 1048576 | tf_op jit(solution)/shard_map/all_to_all | solution.py:304
  572.7 27.6 %copy-start.85 = (u32[32]{0:T(128)S(1)}, u32[32]{0:T(128)}, u32[]{:S(2)}) copy-start(u32[32]{0:T(128)} %constant.126) | copy-start | bytes 388
  572.7 28.8 %copy-start.79 = (f32[512]{0:T(512)S(1)}, f32[512]{0:T(512)}, u32[]{:S(2)}) copy-start(f32[512]{0:T(512)} %get-tuple-element.60) | copy-start | bytes 6148
  572.7 28.8 %copy-start.80 = (f32[512]{0:T(512)S(1)}, f32[512]{0:T(512)}, u32[]{:S(2)}) copy-start(f32[512]{0:T(512)} %get-tuple-element.69) | copy-start | bytes 6148
  596.2 31.2 %all-to-all-start.2 = ((bf16[2,1,256,512]{3,0,1,2:T(2,128)(2,1)}), bf16[2,1,256,512]{3,0,1,2:T(2,128)(2,1)S(1)}, u32[]{:S(2)}, u32[]{:S(2)}) async-start(bf16[2,1,256,512]{3,0,1,2:T(2,128)(2,1)} %copy.185), calls=%async_computation.18 | async-start | bytes 1048576 | tf_op jit(solution)/shard_map/all_to_all | solution.py:307
  (54 other events, 89.2 us)
Sparse Core Ops, SparseCore 0:
  57.9 9.9 reduce-scatter.41
  73.5 10.2 reduce-scatter.33
  93.2 17.1 reduce-scatter.35
  113.1 14.2 reduce-scatter.43
  129.5 12.0 reduce-scatter.57
  180.6 16.6 reduce-scatter.45
  199.5 13.2 reduce-scatter.49
  219.9 16.6 reduce-scatter.37
  238.1 14.9 all-gather.14
  254.5 14.8 all-gather.10
  270.9 11.7 all-gather.8
  285.4 15.7 reduce-scatter.59
  304.0 14.5 reduce-scatter.51
  321.3 14.5 reduce-scatter.47
  349.9 8.5 reduce-scatter.53
  360.5 9.6 reduce-scatter.61
  393.7 9.7 all-gather.12
  405.2 10.7 all-gather.16
  417.6 11.7 all-gather.6
  432.2 15.7 reduce-scatter.55
  450.7 14.5 reduce-scatter.63
  468.2 14.5 reduce-scatter.39
  486.4 67.7 reduce-scatter.65
  557.6 77.6 reduce-scatter.73
  639.4 66.6 reduce-scatter.71
  710.1 66.8 reduce-scatter.69
  780.5 147.9 reduce-scatter.67
  932.5 148.0 reduce-scatter.77
  1084.2 147.9 reduce-scatter.75
